TPU v7x, 256 devices: a whole 4x4x8 slice. The times are simulated.
256 devices in a mesh: grp: 8 (over x, y_hi), blk: 32 (over z, y_lo, core).
Axes of the slice: x: 4, y: 4 (y_hi: 2, y_lo: 2; y = y_hi * 2 + y_lo), z: 8, core: 2. Of those that a mesh axis runs over, the one named last changes fastest.
Arguments:
- counts: int32 [65536, 1024], P(('grp', 'blk')), may hold values from 0 to 5
- tile_live: int32 [512, 8], P(('grp', 'blk')), may hold values from 0 to 1
- doc_lengths: int32 [65536], P(('grp', 'blk')), may hold values from 256 to 4095
- doc_mix: bfloat16 [65536, 4096], P(('grp', 'blk')), may hold values from 0.019897461 to 50
- word_topic: float32 [4096, 4096], P('blk'), may hold values from 0.01 to 8
- topic_total: float32 [4096], replicated, may hold values from 20000 to 400000
Outputs:
- doc_share: bfloat16 [65536, 4096], P(('grp', 'blk'))
- word_topic_new: float32 [4096, 4096], P('blk')
- topic_mean: float32 [4096], replicated
All inputs are finite; a program needn't handle non-finite values.
Results may differ from a plain program's by a relative error of at most 0.0004.
The roundings to bfloat16 on the way count: a program that leaves them out, or rounds other values in their place, can miss the bound.
Values may be sent and summed in bfloat16 or wider, within the bound.
A program may use at most 128 MiB of HBM per device.

v0:
```python
import jax
import jax.numpy as jnp
from jax import lax
from jax.sharding import PartitionSpec as P

VOCAB = 262144
alpha_prior = 0.1
beta_prior = 0.01


def passed_along(block, axis, distance):
    devices = range(lax.axis_size(axis))
    route = [((i - distance) % len(devices), i) for i in devices]
    return lax.ppermute(block, axis, route)


def tile_terms(operands):
    doc_rows, block_counts, visitor = operands
    normalizer = jnp.dot(doc_rows, visitor.T, preferred_element_type=jnp.float32)
    ratio = (block_counts / normalizer).astype(jnp.bfloat16)
    doc_part = jnp.dot(ratio, visitor, preferred_element_type=jnp.float32)
    word_part = jnp.dot(ratio.T, doc_rows, preferred_element_type=jnp.float32)
    return (doc_part, word_part)


def shard_terms(visitor, block_counts, doc_low):
    return tile_terms((doc_low, block_counts, visitor))


def local(counts, tile_live, doc_lengths, doc_mix, word_topic, topic_total):
    block_rows = word_topic.shape[0]
    visits = tile_live.shape[1]
    word_weight = (word_topic + beta_prior) / (topic_total + beta_prior * VOCAB)[None, :]
    word_low = word_weight.astype(jnp.bfloat16)
    mix_wide = doc_mix.astype(jnp.float32)
    doc_theta = mix_wide / jnp.sum(mix_wide, axis=1, keepdims=True)
    doc_weight = doc_lengths.astype(jnp.float32)[:, None] * doc_theta + alpha_prior
    doc_low = doc_weight.astype(jnp.bfloat16)
    live_full = jnp.repeat(jnp.repeat(tile_live, block_rows, axis=0), block_rows, axis=1)
    live_counts = counts.astype(jnp.float32) * live_full.astype(jnp.float32)
    window_len = jnp.sum(live_counts, axis=1)
    doc_proj = jnp.zeros((doc_low.shape[0], doc_low.shape[1]), jnp.float32)
    word_accum = jnp.zeros((block_rows, doc_low.shape[1]), jnp.float32)
    visitor = word_low
    for offset in range(visits):
        if offset > 0:
            visitor, word_accum = (
                passed_along(visitor.astype(jnp.float32), "blk", -1).astype(visitor.dtype),
                passed_along(word_accum, "blk", -1),
            )
        block_counts = live_counts[:, offset * block_rows : (offset + 1) * block_rows]
        doc_part, word_part = shard_terms(visitor, block_counts, doc_low)
        doc_proj = doc_proj + doc_part
        word_accum = word_accum + word_part
    word_accum = passed_along(word_accum, "blk", visits - 1)
    doc_new = doc_weight * doc_proj
    column_sum = jnp.sum(doc_new, axis=0)
    topic_count = doc_low.shape[1]
    doc_share = (
        topic_count * (doc_new + alpha_prior) / (window_len[:, None] + topic_count * alpha_prior)
    ).astype(jnp.bfloat16)
    word_sum = lax.psum(word_accum, "grp")
    topic_sum = lax.psum(column_sum, ("grp", "blk"))
    vocab_window = block_rows * lax.axis_size("blk")
    return (doc_share, word_weight * word_sum, topic_sum / vocab_window)


def solution(mesh):
    return jax.shard_map(
        local,
        mesh=mesh,
        in_specs=(
            P(("grp", "blk"), None),
            P(("grp", "blk"), None),
            P(("grp", "blk")),
            P(("grp", "blk"), None),
            P("blk", None),
            P(),
        ),
        out_specs=(P(("grp", "blk"), None), P("blk", None), P()),
        check_vma=False,
    )
```

profile of v0, /device:TPU:161, one launch (start us, length us, event | category | flops | bytes accessed | tf_op | source)
XLA Modules:
  0.0 519.2 jit_solution(7656554678656352072)
XLA Ops:
  7.2 0.8 convert_element_type.95
  8.1 2.0 convert_reduce_fusion
  10.0 0.7 broadcast_add_fusion
  10.7 1.0 fusion.8
  12.4 1.0 copy-done
  13.7 0.7 fusion.9
  14.8 0.8 collective-permute-start.7
  15.6 1.5 collective-permute-start
  17.1 34.7 %collective-permute-done = bf16[128,4096]{1,0:T(8,128)(2,1)S(1)} collective-permute-done((bf16[128,4096]{1,0:T(8,128)(2,1)S(1)}, bf16[128,4096]{1,0:T(8,128)(2,1)S(1)}, u32[]{:S(2)}, u32[]{:S(2)}) %collective-permute-start) | collective-permute-done | bytes 1048608 | tf_op jit(solution)/shard_map/ppermute | solution.py:14
  51.7 0.7 fusion.10
  52.5 0.5 convolution_add_fusion.2
  53.2 2.8 collective-permute-start.1
  56.0 33.8 %collective-permute-done.1 = bf16[128,4096]{1,0:T(8,128)(2,1)S(1)} collective-permute-done((bf16[128,4096]{1,0:T(8,128)(2,1)S(1)}, bf16[128,4096]{1,0:T(8,128)(2,1)S(1)}, u32[]{:S(2)}, u32[]{:S(2)}) %collective-permute-start.1) | collective-permute-done | bytes 1048608 | tf_op jit(solution)/shard_map/ppermute | solution.py:14
  89.8 0.7 fusion.11
  90.5 0.5 fusion.42
  91.3 1.1 collective-permute-start.9
  92.4 2.8 collective-permute-start.2
  95.2 32.9 %collective-permute-done.2 = bf16[128,4096]{1,0:T(8,128)(2,1)S(1)} collective-permute-done((bf16[128,4096]{1,0:T(8,128)(2,1)S(1)}, bf16[128,4096]{1,0:T(8,128)(2,1)S(1)}, u32[]{:S(2)}, u32[]{:S(2)}) %collective-permute-start.2) | collective-permute-done | bytes 1048608 | tf_op jit(solution)/shard_map/ppermute | solution.py:14
  128.0 0.7 fusion.12
  129.5 2.0 collective-permute-start.10
  131.5 2.8 collective-permute-start.3
  134.3 32.0 %collective-permute-done.3 = bf16[128,4096]{1,0:T(8,128)(2,1)S(1)} collective-permute-done((bf16[128,4096]{1,0:T(8,128)(2,1)S(1)}, bf16[128,4096]{1,0:T(8,128)(2,1)S(1)}, u32[]{:S(2)}, u32[]{:S(2)}) %collective-permute-start.3) | collective-permute-done | bytes 1048608 | tf_op jit(solution)/shard_map/ppermute | solution.py:14
  166.3 0.7 fusion.13
  167.7 2.9 collective-permute-start.11
  170.6 2.8 collective-permute-start.4
  173.4 31.1 %collective-permute-done.4 = bf16[128,4096]{1,0:T(8,128)(2,1)S(1)} collective-permute-done((bf16[128,4096]{1,0:T(8,128)(2,1)S(1)}, bf16[128,4096]{1,0:T(8,128)(2,1)S(1)}, u32[]{:S(2)}, u32[]{:S(2)}) %collective-permute-start.4) | collective-permute-done | bytes 1048608 | tf_op jit(solution)/shard_map/ppermute | solution.py:14
  204.5 0.7 fusion.14
  206.0 3.8 collective-permute-start.12
  209.8 2.8 collective-permute-start.5
  212.6 30.2 %collective-permute-done.5 = bf16[128,4096]{1,0:T(8,128)(2,1)S(1)} collective-permute-done((bf16[128,4096]{1,0:T(8,128)(2,1)S(1)}, bf16[128,4096]{1,0:T(8,128)(2,1)S(1)}, u32[]{:S(2)}, u32[]{:S(2)}) %collective-permute-start.5) | collective-permute-done | bytes 1048608 | tf_op jit(solution)/shard_map/ppermute | solution.py:14
  242.7 0.7 fusion.15
  244.2 4.7 collective-permute-start.13
  248.9 2.8 collective-permute-start.6
  251.7 0.7 fusion.40
  252.4 28.6 %collective-permute-done.6 = bf16[128,4096]{1,0:T(8,128)(2,1)S(1)} collective-permute-done((bf16[128,4096]{1,0:T(8,128)(2,1)S(1)}, bf16[128,4096]{1,0:T(8,128)(2,1)S(1)}, u32[]{:S(2)}, u32[]{:S(2)}) %collective-permute-start.6) | collective-permute-done | bytes 1048608 | tf_op jit(solution)/shard_map/ppermute | solution.py:14
  281.0 0.7 fusion.16
  282.4 6.9 %collective-permute-start.14 = (f32[128,4096]{1,0:T(8,128)S(1)}, f32[128,4096]{1,0:T(8,128)}, u32[]{:S(2)}, u32[]{:S(2)}) collective-permute-start(f32[128,4096]{1,0:T(8,128)S(1)} %add.96), channel_id=1, source_target_pairs={{25,0},{26,1},{27,2},{28,3},{29,4},{30,5},{31,6},{0,7},{1,8},{2,9}... | collective-permute-start | bytes 6291464 | tf_op jit(solution)/shard_map/ppermute | solution.py:14
  289.3 2.7 convolution_add_fusion.1
  292.0 2.6 fusion.52
  294.6 2.6 fusion.51
  297.2 2.7 fusion.50
  299.9 2.7 fusion.49
  302.6 2.6 fusion.48
  305.2 69.0 %collective-permute-done.14 = f32[128,4096]{1,0:T(8,128)} collective-permute-done((f32[128,4096]{1,0:T(8,128)S(1)}, f32[128,4096]{1,0:T(8,128)}, u32[]{:S(2)}, u32[]{:S(2)}) %collective-permute-start.14) | collective-permute-done | bytes 2097184 | tf_op jit(solution)/shard_map/ppermute | solution.py:14
  374.2 11.5 %fusion.39 = (f32[4096]{0:T(1024)S(1)}, bf16[256,4096]{1,0:T(8,128)(2,1)}) fusion(f32[256]{0:T(256)S(1)} %broadcast_add_fusion.1, f32[256,4096]{1,0:T(8,128)} %fusion.48, f32[256,4096]{1,0:T(8,128)} %fusion.49, f32[256,4096]{1,0:T(8,128)} %fusion.50, f32[256,4096]{1,0:T(8,128)} %fusion.51, f32[256,4096]{1,0:T(8,128)} %fusion.52, ...), kind=kOutput, calls=%fused_computation.64 | convolution fusion | flops 285208576 | bytes 30493696 | tf_op jit(solution)/shard_map/dot_general | solution.py:21
  385.7 122.8 %psum.15 = f32[4096]{0:T(1024)S(1)} all-reduce(f32[4096]{0:T(1024)S(1)} %get-tuple-element.5), channel_id=1, replica_groups=mesh['grp'=8,'blk'=32] {'grp','blk'}, use_global_device_ids=true, to_apply=%region_4.0 | all-reduce | flops 4096 | bytes 32768 | tf_op jit(solution)/shard_map/psum | solution.py:63
  508.5 0.6 broadcast_multiply_fusion
  509.1 3.2 fusion.17
  (36 shorter events, 5.5 us)
Async XLA Ops:
  7.2 3.6 copy-start.1
  7.2 2.8 copy-start.3
  7.2 501.9 %all-reduce.2.cloned.1.call-start = ((), (), s32[]{:S(2)}) async-start(), calls=%async_computation | async-start | bytes 4194304 | tf_op jit(solution)/shard_map/psum | solution.py:62
  10.7 1.4 copy-start.2
  11.8 1.6 copy-start
  14.8 37.6 %collective-permute-start.7 = (f32[128,4096]{1,0:T(8,128)S(1)}, f32[128,4096]{1,0:T(8,128)S(1)}, u32[]{:S(2)}, u32[]{:S(2)}) collective-permute-start(f32[128,4096]{1,0:T(8,128)S(1)} %fusion.41), channel_id=1, source_target_pairs={{1,0},{2,1},{3,2},{4,3},{5,4},{6,5},{7,6},{8,7},{9,8},{10,9},{11,1... | collective-permute-start | bytes 6291464 | tf_op jit(solution)/shard_map/ppermute | solution.py:14
  15.6 36.1 %collective-permute-start = (bf16[128,4096]{1,0:T(8,128)(2,1)S(1)}, bf16[128,4096]{1,0:T(8,128)(2,1)S(1)}, u32[]{:S(2)}, u32[]{:S(2)}) collective-permute-start(bf16[128,4096]{1,0:T(8,128)(2,1)S(1)} %fusion.18), channel_id=1, source_target_pairs={{1,0},{2,1},{3,2},{4,3},{5,4},{6,5},{7,6},{8,7},{9,8},{10,9},{11,1... | collective-permute-start | bytes 3145736 | tf_op jit(solution)/shard_map/ppermute | solution.py:14
  53.0 38.0 %collective-permute-start.8 = (f32[128,4096]{1,0:T(8,128)S(1)}, f32[128,4096]{1,0:T(8,128)S(1)}, u32[]{:S(2)}, u32[]{:S(2)}) collective-permute-start(f32[128,4096]{1,0:T(8,128)S(1)} %convolution_add_fusion.2), channel_id=1, source_target_pairs={{1,0},{2,1},{3,2},{4,3},{5,4},{6,5},{7,6},{8,7},{9,8},{10,9},{11,1... | collective-permute-start | bytes 6291464 | tf_op jit(solution)/shard_map/ppermute | solution.py:14
  53.2 36.6 %collective-permute-start.1 = (bf16[128,4096]{1,0:T(8,128)(2,1)S(1)}, bf16[128,4096]{1,0:T(8,128)(2,1)S(1)}, u32[]{:S(2)}, u32[]{:S(2)}) collective-permute-start(bf16[128,4096]{1,0:T(8,128)(2,1)S(1)} %collective-permute-done), channel_id=1, source_target_pairs={{1,0},{2,1},{3,2},{4,3},{5,4},{6,5},{7,6},{8,7},{9,8},{10,9},{11,1... | collective-permute-start | bytes 3145736 | tf_op jit(solution)/shard_map/ppermute | solution.py:14
  91.3 38.0 %collective-permute-start.9 = (f32[128,4096]{1,0:T(8,128)S(1)}, f32[128,4096]{1,0:T(8,128)S(1)}, u32[]{:S(2)}, u32[]{:S(2)}) collective-permute-start(f32[128,4096]{1,0:T(8,128)S(1)} %add.91), channel_id=1, source_target_pairs={{1,0},{2,1},{3,2},{4,3},{5,4},{6,5},{7,6},{8,7},{9,8},{10,9},{11,1... | collective-permute-start | bytes 6291464 | tf_op jit(solution)/shard_map/ppermute | solution.py:14
  92.4 35.7 %collective-permute-start.2 = (bf16[128,4096]{1,0:T(8,128)(2,1)S(1)}, bf16[128,4096]{1,0:T(8,128)(2,1)S(1)}, u32[]{:S(2)}, u32[]{:S(2)}) collective-permute-start(bf16[128,4096]{1,0:T(8,128)(2,1)S(1)} %collective-permute-done.1), channel_id=1, source_target_pairs={{1,0},{2,1},{3,2},{4,3},{5,4},{6,5},{7,6},{8,7},{9,8},{10,9},{11,1... | collective-permute-start | bytes 3145736 | tf_op jit(solution)/shard_map/ppermute | solution.py:14
  129.5 38.0 %collective-permute-start.10 = (f32[128,4096]{1,0:T(8,128)S(1)}, f32[128,4096]{1,0:T(8,128)S(1)}, u32[]{:S(2)}, u32[]{:S(2)}) collective-permute-start(f32[128,4096]{1,0:T(8,128)S(1)} %add.92), channel_id=1, source_target_pairs={{1,0},{2,1},{3,2},{4,3},{5,4},{6,5},{7,6},{8,7},{9,8},{10,9},{11,1... | collective-permute-start | bytes 6291464 | tf_op jit(solution)/shard_map/ppermute | solution.py:14
  131.5 34.8 %collective-permute-start.3 = (bf16[128,4096]{1,0:T(8,128)(2,1)S(1)}, bf16[128,4096]{1,0:T(8,128)(2,1)S(1)}, u32[]{:S(2)}, u32[]{:S(2)}) collective-permute-start(bf16[128,4096]{1,0:T(8,128)(2,1)S(1)} %collective-permute-done.2), channel_id=1, source_target_pairs={{1,0},{2,1},{3,2},{4,3},{5,4},{6,5},{7,6},{8,7},{9,8},{10,9},{11,1... | collective-permute-start | bytes 3145736 | tf_op jit(solution)/shard_map/ppermute | solution.py:14
  167.7 38.0 %collective-permute-start.11 = (f32[128,4096]{1,0:T(8,128)S(1)}, f32[128,4096]{1,0:T(8,128)S(1)}, u32[]{:S(2)}, u32[]{:S(2)}) collective-permute-start(f32[128,4096]{1,0:T(8,128)S(1)} %add.93), channel_id=1, source_target_pairs={{1,0},{2,1},{3,2},{4,3},{5,4},{6,5},{7,6},{8,7},{9,8},{10,9},{11,1... | collective-permute-start | bytes 6291464 | tf_op jit(solution)/shard_map/ppermute | solution.py:14
  170.6 33.9 %collective-permute-start.4 = (bf16[128,4096]{1,0:T(8,128)(2,1)S(1)}, bf16[128,4096]{1,0:T(8,128)(2,1)S(1)}, u32[]{:S(2)}, u32[]{:S(2)}) collective-permute-start(bf16[128,4096]{1,0:T(8,128)(2,1)S(1)} %collective-permute-done.3), channel_id=1, source_target_pairs={{1,0},{2,1},{3,2},{4,3},{5,4},{6,5},{7,6},{8,7},{9,8},{10,9},{11,1... | collective-permute-start | bytes 3145736 | tf_op jit(solution)/shard_map/ppermute | solution.py:14
  206.0 38.0 %collective-permute-start.12 = (f32[128,4096]{1,0:T(8,128)S(1)}, f32[128,4096]{1,0:T(8,128)S(1)}, u32[]{:S(2)}, u32[]{:S(2)}) collective-permute-start(f32[128,4096]{1,0:T(8,128)S(1)} %add.94), channel_id=1, source_target_pairs={{1,0},{2,1},{3,2},{4,3},{5,4},{6,5},{7,6},{8,7},{9,8},{10,9},{11,1... | collective-permute-start | bytes 6291464 | tf_op jit(solution)/shard_map/ppermute | solution.py:14
  209.8 33.0 %collective-permute-start.5 = (bf16[128,4096]{1,0:T(8,128)(2,1)S(1)}, bf16[128,4096]{1,0:T(8,128)(2,1)S(1)}, u32[]{:S(2)}, u32[]{:S(2)}) collective-permute-start(bf16[128,4096]{1,0:T(8,128)(2,1)S(1)} %collective-permute-done.4), channel_id=1, source_target_pairs={{1,0},{2,1},{3,2},{4,3},{5,4},{6,5},{7,6},{8,7},{9,8},{10,9},{11,1... | collective-permute-start | bytes 3145736 | tf_op jit(solution)/shard_map/ppermute | solution.py:14
  244.2 38.0 %collective-permute-start.13 = (f32[128,4096]{1,0:T(8,128)S(1)}, f32[128,4096]{1,0:T(8,128)S(1)}, u32[]{:S(2)}, u32[]{:S(2)}) collective-permute-start(f32[128,4096]{1,0:T(8,128)S(1)} %add.95), channel_id=1, source_target_pairs={{1,0},{2,1},{3,2},{4,3},{5,4},{6,5},{7,6},{8,7},{9,8},{10,9},{11,1... | collective-permute-start | bytes 6291464 | tf_op jit(solution)/shard_map/ppermute | solution.py:14
  248.9 32.1 %collective-permute-start.6 = (bf16[128,4096]{1,0:T(8,128)(2,1)S(1)}, bf16[128,4096]{1,0:T(8,128)(2,1)S(1)}, u32[]{:S(2)}, u32[]{:S(2)}) collective-permute-start(bf16[128,4096]{1,0:T(8,128)(2,1)S(1)} %collective-permute-done.5), channel_id=1, source_target_pairs={{1,0},{2,1},{3,2},{4,3},{5,4},{6,5},{7,6},{8,7},{9,8},{10,9},{11,1... | collective-permute-start | bytes 3145736 | tf_op jit(solution)/shard_map/ppermute | solution.py:14
  282.4 91.8 %collective-permute-start.14 = (f32[128,4096]{1,0:T(8,128)S(1)}, f32[128,4096]{1,0:T(8,128)}, u32[]{:S(2)}, u32[]{:S(2)}) collective-permute-start(f32[128,4096]{1,0:T(8,128)S(1)} %add.96), channel_id=1, source_target_pairs={{25,0},{26,1},{27,2},{28,3},{29,4},{30,5},{31,6},{0,7},{1,8},{2,9}... | collective-permute-start | bytes 6291464 | tf_op jit(solution)/shard_map/ppermute | solution.py:14
Sparse Core Ops, SparseCore 0:
  374.3 117.2 all-reduce.1
where the time goes:
time: 520 us; the launch traced here: 519 us
  waiting for transfers between devices  292 us (56%)
  blocking collectives  123 us (24%)
  starting transfers between devices  40.6 us (8%)
  matrix products  37.6 us (7%)
  between operations  14.3 us (3%)
  other arithmetic  10.4 us (2%)
    ppermute x15, waiting for transfers between devices, passed_along(): return lax.ppermute(block, axis, route)  292 us
    psum x1, blocking collectives, local(): topic_sum = lax.psum(column_sum, ('grp', 'blk'))  123 us
    ppermute x15, starting transfers between devices, passed_along(): return lax.ppermute(block, axis, route)  40.6 us
    dot_general x8, matrix products, tile_terms(): doc_part = jnp.dot(ratio, visitor, preferred_element_type=jnp.float32)  28.1 us
  transfers between devices with their start and end apart: 16, of which 8 were waited for; matrix products, arithmetic and copies ran while one was open for 7% of the time, Pallas kernels for 0%

commit v1 on v0

--- a/solution.py
+++ b/solution.py
@@ -60,7 +60,7 @@
         topic_count * (doc_new + alpha_prior) / (window_len[:, None] + topic_count * alpha_prior)
     ).astype(jnp.bfloat16)
     word_sum = lax.psum(word_accum, "grp")
-    topic_sum = lax.psum(column_sum, ("grp", "blk"))
+    topic_sum = lax.psum(lax.psum(column_sum, "blk"), "grp")
     vocab_window = block_rows * lax.axis_size("blk")
     return (doc_share, word_weight * word_sum, topic_sum / vocab_window)
 

time: 520 us -> 552 us (1.062)
  the two profiles are of different devices: /device:TPU:161 before, /device:TPU:0 now
where the time goes in v1:
time: 552 us
  waiting for transfers between devices  294 us (53%)
  blocking collectives  163 us (30%)
  matrix products  37.6 us (7%)
  starting transfers between devices  31 us (6%)
  between operations  14.3 us (3%)
  other arithmetic  10.4 us (2%)
    ppermute x15, waiting for transfers between devices, passed_along(): return lax.ppermute(block, axis, route)  294 us
    psum x2, blocking collectives, local(): topic_sum = lax.psum(lax.psum(column_sum, 'blk'), 'grp')  163 us
    ppermute x15, starting transfers between devices, passed_along(): return lax.ppermute(block, axis, route)  31 us
    dot_general x8, matrix products, tile_terms(): doc_part = jnp.dot(ratio, visitor, preferred_element_type=jnp.float32)  28.1 us
  transfers between devices with their start and end apart: 16, of which 8 were waited for; matrix products, arithmetic and copies ran while one was open for 7% of the time, Pallas kernels for 0%

profile of v1, /device:TPU:0, one launch (start us, length us, event | category | flops | bytes accessed | tf_op | source)
XLA Modules:
  0.0 551.9 jit_solution(11187060426019494073)
XLA Ops:
  7.2 0.8 convert_element_type.95
  8.1 2.0 convert_reduce_fusion
  10.0 0.7 broadcast_add_fusion
  10.7 1.0 fusion.8
  12.4 1.0 copy-done
  13.7 0.7 fusion.9
  14.4 0.5 fusion.41
  14.9 4.7 collective-permute-start.7
  19.5 0.7 collective-permute-start
  20.2 34.1 %collective-permute-done = bf16[128,4096]{1,0:T(8,128)(2,1)S(1)} collective-permute-done((bf16[128,4096]{1,0:T(8,128)(2,1)S(1)}, bf16[128,4096]{1,0:T(8,128)(2,1)S(1)}, u32[]{:S(2)}, u32[]{:S(2)}) %collective-permute-start) | collective-permute-done | bytes 1048608 | tf_op jit(solution)/shard_map/ppermute | solution.py:14
  54.3 0.7 fusion.10
  55.0 0.5 convolution_add_fusion.2
  55.6 4.1 collective-permute-start.8
  59.8 34.7 %collective-permute-done.1 = bf16[128,4096]{1,0:T(8,128)(2,1)S(1)} collective-permute-done((bf16[128,4096]{1,0:T(8,128)(2,1)S(1)}, bf16[128,4096]{1,0:T(8,128)(2,1)S(1)}, u32[]{:S(2)}, u32[]{:S(2)}) %collective-permute-start.1) | collective-permute-done | bytes 1048608 | tf_op jit(solution)/shard_map/ppermute | solution.py:14
  94.5 0.7 fusion.11
  95.2 0.5 fusion.42
  95.9 4.1 collective-permute-start.9
  100.1 34.7 %collective-permute-done.2 = bf16[128,4096]{1,0:T(8,128)(2,1)S(1)} collective-permute-done((bf16[128,4096]{1,0:T(8,128)(2,1)S(1)}, bf16[128,4096]{1,0:T(8,128)(2,1)S(1)}, u32[]{:S(2)}, u32[]{:S(2)}) %collective-permute-start.2) | collective-permute-done | bytes 1048608 | tf_op jit(solution)/shard_map/ppermute | solution.py:14
  134.8 0.7 fusion.12
  135.5 0.5 fusion.43
  136.3 4.1 collective-permute-start.10
  140.7 34.5 %collective-permute-done.3 = bf16[128,4096]{1,0:T(8,128)(2,1)S(1)} collective-permute-done((bf16[128,4096]{1,0:T(8,128)(2,1)S(1)}, bf16[128,4096]{1,0:T(8,128)(2,1)S(1)}, u32[]{:S(2)}, u32[]{:S(2)}) %collective-permute-start.3) | collective-permute-done | bytes 1048608 | tf_op jit(solution)/shard_map/ppermute | solution.py:14
  175.2 0.7 fusion.13
  175.9 0.5 fusion.44
  176.6 4.1 collective-permute-start.11
  180.8 34.7 %collective-permute-done.4 = bf16[128,4096]{1,0:T(8,128)(2,1)S(1)} collective-permute-done((bf16[128,4096]{1,0:T(8,128)(2,1)S(1)}, bf16[128,4096]{1,0:T(8,128)(2,1)S(1)}, u32[]{:S(2)}, u32[]{:S(2)}) %collective-permute-start.4) | collective-permute-done | bytes 1048608 | tf_op jit(solution)/shard_map/ppermute | solution.py:14
  215.5 0.7 fusion.14
  217.0 4.1 collective-permute-start.12
  221.2 34.7 %collective-permute-done.5 = bf16[128,4096]{1,0:T(8,128)(2,1)S(1)} collective-permute-done((bf16[128,4096]{1,0:T(8,128)(2,1)S(1)}, bf16[128,4096]{1,0:T(8,128)(2,1)S(1)}, u32[]{:S(2)}, u32[]{:S(2)}) %collective-permute-start.5) | collective-permute-done | bytes 1048608 | tf_op jit(solution)/shard_map/ppermute | solution.py:14
  255.9 0.7 fusion.15
  256.6 0.5 fusion.46
  257.3 4.1 collective-permute-start.13
  261.5 0.7 fusion.40
  262.2 34.0 %collective-permute-done.6 = bf16[128,4096]{1,0:T(8,128)(2,1)S(1)} collective-permute-done((bf16[128,4096]{1,0:T(8,128)(2,1)S(1)}, bf16[128,4096]{1,0:T(8,128)(2,1)S(1)}, u32[]{:S(2)}, u32[]{:S(2)}) %collective-permute-start.6) | collective-permute-done | bytes 1048608 | tf_op jit(solution)/shard_map/ppermute | solution.py:14
  296.2 0.7 fusion.16
  296.9 0.5 fusion.47
  298.0 2.7 convolution_add_fusion.1
  300.6 2.6 fusion.52
  303.3 2.6 fusion.51
  305.9 2.7 fusion.50
  308.6 2.7 fusion.49
  311.2 2.6 fusion.48
  313.9 52.7 %collective-permute-done.14 = f32[128,4096]{1,0:T(8,128)} collective-permute-done((f32[128,4096]{1,0:T(8,128)S(1)}, f32[128,4096]{1,0:T(8,128)}, u32[]{:S(2)}, u32[]{:S(2)}) %collective-permute-start.14) | collective-permute-done | bytes 2097184 | tf_op jit(solution)/shard_map/ppermute | solution.py:14
  366.6 11.5 %fusion.39 = (f32[4096]{0:T(1024)S(1)}, bf16[256,4096]{1,0:T(8,128)(2,1)}) fusion(f32[256]{0:T(256)S(1)} %broadcast_add_fusion.1, f32[256,4096]{1,0:T(8,128)} %fusion.48, f32[256,4096]{1,0:T(8,128)} %fusion.49, f32[256,4096]{1,0:T(8,128)} %fusion.50, f32[256,4096]{1,0:T(8,128)} %fusion.51, f32[256,4096]{1,0:T(8,128)} %fusion.52, ...), kind=kOutput, calls=%fused_computation.64 | convolution fusion | flops 285208576 | bytes 30493696 | tf_op jit(solution)/shard_map/dot_general | solution.py:21
  378.1 118.5 %psum.22 = f32[4096]{0:T(1024)S(1)} all-reduce(f32[4096]{0:T(1024)S(1)} %get-tuple-element.5), channel_id=1, replica_groups=mesh['grp'=8,'blk'=32] {'blk'}, use_global_device_ids=true, to_apply=%region_4.0 | all-reduce | flops 4096 | bytes 32768 | tf_op jit(solution)/shard_map/psum | solution.py:63
  496.5 44.7 %psum.23 = f32[4096]{0:T(1024)S(1)} all-reduce(f32[4096]{0:T(1024)S(1)} %psum.22), channel_id=1, replica_groups=mesh['grp'=8,'blk'=32] {'grp'}, use_global_device_ids=true, to_apply=%region_5.0 | all-reduce | flops 4096 | bytes 32768 | tf_op jit(solution)/shard_map/psum | solution.py:63
  541.2 0.6 broadcast_multiply_fusion
  541.9 3.2 fusion.17
  (37 shorter events, 4.0 us)
Async XLA Ops:
  7.2 3.6 copy-start.1
  7.2 2.8 copy-start.3
  7.2 534.7 %all-reduce.2.cloned.1.call-start = ((), (), s32[]{:S(2)}) async-start(), calls=%async_computation | async-start | bytes 4194304 | tf_op jit(solution)/shard_map/psum | solution.py:62
  10.7 1.4 copy-start.2
  11.8 1.6 copy-start
  14.9 40.2 %collective-permute-start.7 = (f32[128,4096]{1,0:T(8,128)S(1)}, f32[128,4096]{1,0:T(8,128)S(1)}, u32[]{:S(2)}, u32[]{:S(2)}) collective-permute-start(f32[128,4096]{1,0:T(8,128)S(1)} %fusion.41), channel_id=1, source_target_pairs={{1,0},{2,1},{3,2},{4,3},{5,4},{6,5},{7,6},{8,7},{9,8},{10,9},{11,1... | collective-permute-start | bytes 6291464 | tf_op jit(solution)/shard_map/ppermute | solution.py:14
  19.5 34.8 %collective-permute-start = (bf16[128,4096]{1,0:T(8,128)(2,1)S(1)}, bf16[128,4096]{1,0:T(8,128)(2,1)S(1)}, u32[]{:S(2)}, u32[]{:S(2)}) collective-permute-start(bf16[128,4096]{1,0:T(8,128)(2,1)S(1)} %fusion.18), channel_id=1, source_target_pairs={{1,0},{2,1},{3,2},{4,3},{5,4},{6,5},{7,6},{8,7},{9,8},{10,9},{11,1... | collective-permute-start | bytes 3145736 | tf_op jit(solution)/shard_map/ppermute | solution.py:14
  55.6 40.1 %collective-permute-start.8 = (f32[128,4096]{1,0:T(8,128)S(1)}, f32[128,4096]{1,0:T(8,128)S(1)}, u32[]{:S(2)}, u32[]{:S(2)}) collective-permute-start(f32[128,4096]{1,0:T(8,128)S(1)} %convolution_add_fusion.2), channel_id=1, source_target_pairs={{1,0},{2,1},{3,2},{4,3},{5,4},{6,5},{7,6},{8,7},{9,8},{10,9},{11,1... | collective-permute-start | bytes 6291464 | tf_op jit(solution)/shard_map/ppermute | solution.py:14
  59.7 34.8 %collective-permute-start.1 = (bf16[128,4096]{1,0:T(8,128)(2,1)S(1)}, bf16[128,4096]{1,0:T(8,128)(2,1)S(1)}, u32[]{:S(2)}, u32[]{:S(2)}) collective-permute-start(bf16[128,4096]{1,0:T(8,128)(2,1)S(1)} %collective-permute-done), channel_id=1, source_target_pairs={{1,0},{2,1},{3,2},{4,3},{5,4},{6,5},{7,6},{8,7},{9,8},{10,9},{11,1... | collective-permute-start | bytes 3145736 | tf_op jit(solution)/shard_map/ppermute | solution.py:14
  95.9 40.1 %collective-permute-start.9 = (f32[128,4096]{1,0:T(8,128)S(1)}, f32[128,4096]{1,0:T(8,128)S(1)}, u32[]{:S(2)}, u32[]{:S(2)}) collective-permute-start(f32[128,4096]{1,0:T(8,128)S(1)} %add.93), channel_id=1, source_target_pairs={{1,0},{2,1},{3,2},{4,3},{5,4},{6,5},{7,6},{8,7},{9,8},{10,9},{11,1... | collective-permute-start | bytes 6291464 | tf_op jit(solution)/shard_map/ppermute | solution.py:14
  100.0 34.8 %collective-permute-start.2 = (bf16[128,4096]{1,0:T(8,128)(2,1)S(1)}, bf16[128,4096]{1,0:T(8,128)(2,1)S(1)}, u32[]{:S(2)}, u32[]{:S(2)}) collective-permute-start(bf16[128,4096]{1,0:T(8,128)(2,1)S(1)} %collective-permute-done.1), channel_id=1, source_target_pairs={{1,0},{2,1},{3,2},{4,3},{5,4},{6,5},{7,6},{8,7},{9,8},{10,9},{11,1... | collective-permute-start | bytes 3145736 | tf_op jit(solution)/shard_map/ppermute | solution.py:14
  136.3 40.1 %collective-permute-start.10 = (f32[128,4096]{1,0:T(8,128)S(1)}, f32[128,4096]{1,0:T(8,128)S(1)}, u32[]{:S(2)}, u32[]{:S(2)}) collective-permute-start(f32[128,4096]{1,0:T(8,128)S(1)} %add.94), channel_id=1, source_target_pairs={{1,0},{2,1},{3,2},{4,3},{5,4},{6,5},{7,6},{8,7},{9,8},{10,9},{11,1... | collective-permute-start | bytes 6291464 | tf_op jit(solution)/shard_map/ppermute | solution.py:14
  140.4 34.8 %collective-permute-start.3 = (bf16[128,4096]{1,0:T(8,128)(2,1)S(1)}, bf16[128,4096]{1,0:T(8,128)(2,1)S(1)}, u32[]{:S(2)}, u32[]{:S(2)}) collective-permute-start(bf16[128,4096]{1,0:T(8,128)(2,1)S(1)} %collective-permute-done.2), channel_id=1, source_target_pairs={{1,0},{2,1},{3,2},{4,3},{5,4},{6,5},{7,6},{8,7},{9,8},{10,9},{11,1... | collective-permute-start | bytes 3145736 | tf_op jit(solution)/shard_map/ppermute | solution.py:14
  176.6 40.1 %collective-permute-start.11 = (f32[128,4096]{1,0:T(8,128)S(1)}, f32[128,4096]{1,0:T(8,128)S(1)}, u32[]{:S(2)}, u32[]{:S(2)}) collective-permute-start(f32[128,4096]{1,0:T(8,128)S(1)} %add.95), channel_id=1, source_target_pairs={{1,0},{2,1},{3,2},{4,3},{5,4},{6,5},{7,6},{8,7},{9,8},{10,9},{11,1... | collective-permute-start | bytes 6291464 | tf_op jit(solution)/shard_map/ppermute | solution.py:14
  180.7 34.8 %collective-permute-start.4 = (bf16[128,4096]{1,0:T(8,128)(2,1)S(1)}, bf16[128,4096]{1,0:T(8,128)(2,1)S(1)}, u32[]{:S(2)}, u32[]{:S(2)}) collective-permute-start(bf16[128,4096]{1,0:T(8,128)(2,1)S(1)} %collective-permute-done.3), channel_id=1, source_target_pairs={{1,0},{2,1},{3,2},{4,3},{5,4},{6,5},{7,6},{8,7},{9,8},{10,9},{11,1... | collective-permute-start | bytes 3145736 | tf_op jit(solution)/shard_map/ppermute | solution.py:14
  217.0 40.1 %collective-permute-start.12 = (f32[128,4096]{1,0:T(8,128)S(1)}, f32[128,4096]{1,0:T(8,128)S(1)}, u32[]{:S(2)}, u32[]{:S(2)}) collective-permute-start(f32[128,4096]{1,0:T(8,128)S(1)} %add.96), channel_id=1, source_target_pairs={{1,0},{2,1},{3,2},{4,3},{5,4},{6,5},{7,6},{8,7},{9,8},{10,9},{11,1... | collective-permute-start | bytes 6291464 | tf_op jit(solution)/shard_map/ppermute | solution.py:14
  221.1 34.8 %collective-permute-start.5 = (bf16[128,4096]{1,0:T(8,128)(2,1)S(1)}, bf16[128,4096]{1,0:T(8,128)(2,1)S(1)}, u32[]{:S(2)}, u32[]{:S(2)}) collective-permute-start(bf16[128,4096]{1,0:T(8,128)(2,1)S(1)} %collective-permute-done.4), channel_id=1, source_target_pairs={{1,0},{2,1},{3,2},{4,3},{5,4},{6,5},{7,6},{8,7},{9,8},{10,9},{11,1... | collective-permute-start | bytes 3145736 | tf_op jit(solution)/shard_map/ppermute | solution.py:14
  257.3 40.1 %collective-permute-start.13 = (f32[128,4096]{1,0:T(8,128)S(1)}, f32[128,4096]{1,0:T(8,128)S(1)}, u32[]{:S(2)}, u32[]{:S(2)}) collective-permute-start(f32[128,4096]{1,0:T(8,128)S(1)} %add.97), channel_id=1, source_target_pairs={{1,0},{2,1},{3,2},{4,3},{5,4},{6,5},{7,6},{8,7},{9,8},{10,9},{11,1... | collective-permute-start | bytes 6291464 | tf_op jit(solution)/shard_map/ppermute | solution.py:14
  261.4 34.8 %collective-permute-start.6 = (bf16[128,4096]{1,0:T(8,128)(2,1)S(1)}, bf16[128,4096]{1,0:T(8,128)(2,1)S(1)}, u32[]{:S(2)}, u32[]{:S(2)}) collective-permute-start(bf16[128,4096]{1,0:T(8,128)(2,1)S(1)} %collective-permute-done.5), channel_id=1, source_target_pairs={{1,0},{2,1},{3,2},{4,3},{5,4},{6,5},{7,6},{8,7},{9,8},{10,9},{11,1... | collective-permute-start | bytes 3145736 | tf_op jit(solution)/shard_map/ppermute | solution.py:14
  297.7 68.9 %collective-permute-start.14 = (f32[128,4096]{1,0:T(8,128)S(1)}, f32[128,4096]{1,0:T(8,128)}, u32[]{:S(2)}, u32[]{:S(2)}) collective-permute-start(f32[128,4096]{1,0:T(8,128)S(1)} %add.98), channel_id=1, source_target_pairs={{25,0},{26,1},{27,2},{28,3},{29,4},{30,5},{31,6},{0,7},{1,8},{2,9}... | collective-permute-start | bytes 6291464 | tf_op jit(solution)/shard_map/ppermute | solution.py:14
Sparse Core Ops, SparseCore 0:
  366.7 128.5 all-reduce.1
